TPU v7x, 512 devices: a whole 4x4x16 slice. The times are simulated.
512 devices in a mesh: row: 8 (over z_hi, core), col: 16 (over y, z_lo), depth: 4 (over x).
Axes of the slice: x: 4, y: 4, z: 16 (z_hi: 4, z_lo: 4; z = z_hi * 4 + z_lo), core: 2. Of those that a mesh axis runs over, the one named last changes fastest.
Arguments:
- values: bfloat16 [768, 16, 128, 128], P(('row', 'col')), may hold values from -0.47851562 to 0.47851562
- columns: int32 [768, 16], replicated, may hold values from 0 to 767, as said below
Outputs:
- purified: bfloat16 [768, 16, 128, 128], P(('row', 'col'), 'depth')
Inputs may be any that keep to these rules, and one draw needn't show every extreme that they name: Each block row a names 16 different block columns, a itself among them, all within 8 of a around the cycle of 768 block rows (indices wrap).
All inputs are finite; a program needn't handle non-finite values.
Results may differ from a plain program's by a relative error of at most 0.0047.
Values may be sent and summed in bfloat16 or wider, within the bound.
A program may use at most 128 MiB of HBM per device.

v0:
```python
import jax
import jax.numpy as jnp
from jax import lax
from jax.sharding import PartitionSpec as P

HB = 8


def passed_along(value, axis, by):
    peers = lax.axis_size(axis)
    return lax.ppermute(value, axis, [(i, (i + by) % peers) for i in range(peers)])


def matched_blocks(nearby, band_start, own_cols, target_cols, columns):
    total_blocks = columns.shape[0]
    band_count = nearby.shape[0]
    slot_count = nearby.shape[1]
    partner_cols = jnp.take(columns, own_cols, axis=0)
    same_column = partner_cols[:, :, None, :] == target_cols[:, None, :, None]
    slot_ids = jnp.arange(slot_count, dtype=jnp.int32)
    present = jnp.any(same_column, axis=3)
    chosen = jnp.sum(jnp.where(same_column, slot_ids, 0), axis=3)
    offset = jnp.mod(own_cols - band_start, total_blocks)
    inside = offset < band_count
    usable = inside[:, :, None] & present
    flat_index = jnp.where(
        usable, offset[:, :, None] * slot_count + chosen, band_count * slot_count
    )
    flat_blocks = nearby.reshape(band_count * slot_count, nearby.shape[2], nearby.shape[3])
    return jnp.take(flat_blocks, flat_index, axis=0, mode="fill", fill_value=0)


def local(values, columns):
    own_rows, slot_count, block_size, _ = values.shape
    layers = lax.axis_size("depth")
    quarter = slot_count // layers
    layer_index = lax.axis_index("depth")
    group_index = lax.axis_index(("row", "col"))
    first_row = group_index * own_rows
    own_cols = lax.dynamic_slice_in_dim(columns, first_row, own_rows, 0)
    target_cols = lax.dynamic_slice_in_dim(own_cols, layer_index * quarter, quarter, 1)
    hop_count = (HB + own_rows - 1) // own_rows
    reach_last = HB - (hop_count - 1) * own_rows
    lower_parts = []
    upper_parts = []
    for hop_step in range(1, hop_count + 1):
        edge_rows = own_rows if hop_step < hop_count else reach_last
        from_lower = passed_along(values[own_rows - edge_rows :], ("row", "col"), hop_step)
        from_upper = passed_along(values[:edge_rows], ("row", "col"), -hop_step)
        lower_parts.insert(0, from_lower)
        upper_parts.append(from_upper)
    below_rows = jnp.concatenate(lower_parts, axis=0)
    above_rows = jnp.concatenate(upper_parts, axis=0)
    nearby = jnp.concatenate([below_rows, values, above_rows], axis=0)
    selected = matched_blocks(nearby, first_row - HB, own_cols, target_cols, columns)
    square32 = jnp.einsum("aixy,aijyz->ajxz", values, selected, preferred_element_type=jnp.float32)
    square = square32.astype(jnp.bfloat16)
    whole_square = lax.all_gather(square, "depth", axis=1, tiled=True)
    cube32 = jnp.einsum(
        "aixy,aijyz->ajxz", whole_square, selected, preferred_element_type=jnp.float32
    )
    return (3.0 * square32 - 2.0 * cube32).astype(jnp.bfloat16)


def solution(mesh):
    placed = (P(("row", "col"), None, None, None), P())
    return jax.shard_map(
        local,
        mesh=mesh,
        in_specs=placed,
        out_specs=P(("row", "col"), "depth", None, None),
        check_vma=False,
    )
```

profile of v0, /device:TPU:1, one launch (start us, length us, event | category | flops | bytes accessed | tf_op | source)
XLA Modules:
  0.0 335.9 jit_solution(13076159911926167194)
XLA Ops:
  6.5 4.6 %collective-permute-start.1 = (bf16[6,16,128,128]{3,2,1,0:T(8,128)(2,1)}, bf16[6,16,128,128]{3,2,1,0:T(8,128)(2,1)}, u32[]{:S(2)}, u32[]{:S(2)}) collective-permute-start(bf16[6,16,128,128]{3,2,1,0:T(8,128)(2,1)} %param.2), channel_id=1, source_target_pairs={{0,4},{4,8},{8,12},{12,16},{16,20},{20,24},{24,28},{28,32},{32,36}... | collective-permute-start | bytes 9437192 | tf_op jit(solution)/shard_map/ppermute | solution.py:11
  11.2 7.6 %collective-permute-start.2 = (bf16[6,16,128,128]{3,2,1,0:T(8,128)(2,1)}, bf16[6,16,128,128]{3,2,1,0:T(8,128)(2,1)}, u32[]{:S(2)}, u32[]{:S(2)}) collective-permute-start(bf16[6,16,128,128]{3,2,1,0:T(8,128)(2,1)} %param.2), channel_id=1, source_target_pairs={{0,508},{4,0},{8,4},{12,8},{16,12},{20,16},{24,20},{28,24},{32,28}... | collective-permute-start | bytes 9437192 | tf_op jit(solution)/shard_map/ppermute | solution.py:11
  18.8 3.2 fusion.18
  22.0 1.9 collective-permute-start
  23.9 6.7 %collective-permute-start.3 = (bf16[2,16,128,128]{3,2,1,0:T(8,128)(2,1)}, bf16[2,16,128,128]{3,2,1,0:T(8,128)(2,1)}, u32[]{:S(2)}, u32[]{:S(2)}) collective-permute-start(bf16[2,16,128,128]{3,2,1,0:T(8,128)(2,1)} %get-tuple-element.7), channel_id=1, source_target_pairs={{0,504},{4,508},{8,0},{12,4},{16,8},{20,12},{24,16},{28,20},{32,24... | collective-permute-start | bytes 3145736 | tf_op jit(solution)/shard_map/ppermute | solution.py:11
  30.6 1.0 copy.39
  33.3 1.4 dynamic_slice.7
  34.7 0.8 copy.41
  35.5 1.2 gather_fusion
  36.7 0.9 broadcast_select_fusion.7
  39.1 138.4 %collective-permute-done = bf16[2,16,128,128]{3,2,1,0:T(8,128)(2,1)} collective-permute-done((bf16[2,16,128,128]{3,2,1,0:T(8,128)(2,1)}, bf16[2,16,128,128]{3,2,1,0:T(8,128)(2,1)}, u32[]{:S(2)}, u32[]{:S(2)}) %collective-permute-start) | collective-permute-done | bytes 1048608 | tf_op jit(solution)/shard_map/ppermute | solution.py:11
  177.5 2.4 constant_dynamic-update-slice_fusion.4
  179.8 3.9 %constant_dynamic-update-slice_fusion.3 = bf16[22,16,128,128]{3,2,1,0:T(8,128)(2,1)} fusion(bf16[22,16,128,128]{3,2,1,0:T(8,128)(2,1)} %constant_dynamic-update-slice_fusion.4, bf16[6,16,128,128]{3,2,1,0:T(8,128)(2,1)} %collective-permute-done.1), kind=kLoop, calls=%fused_computation.30 | loop fusion | bytes 6291456
  183.8 2.1 constant_dynamic-update-slice_fusion.2
  185.9 4.0 %constant_dynamic-update-slice_fusion.1 = bf16[22,16,128,128]{3,2,1,0:T(8,128)(2,1)} fusion(bf16[22,16,128,128]{3,2,1,0:T(8,128)(2,1)} %constant_dynamic-update-slice_fusion.2, bf16[6,16,128,128]{3,2,1,0:T(8,128)(2,1)} %collective-permute-done.2), kind=kLoop, calls=%fused_computation.28 | loop fusion | bytes 6291456
  189.8 50.2 %collective-permute-done.3 = bf16[2,16,128,128]{3,2,1,0:T(8,128)(2,1)} collective-permute-done((bf16[2,16,128,128]{3,2,1,0:T(8,128)(2,1)}, bf16[2,16,128,128]{3,2,1,0:T(8,128)(2,1)}, u32[]{:S(2)}, u32[]{:S(2)}) %collective-permute-start.3) | collective-permute-done | bytes 1048608 | tf_op jit(solution)/shard_map/ppermute | solution.py:11
  240.1 2.3 constant_dynamic-update-slice_fusion
  242.4 15.5 %gather_fusion.1 = bf16[384,128,128]{2,1,0:T(8,128)(2,1)} fusion(bf16[352,128,128]{2,1,0:T(8,128)(2,1)} %bitcast.1, s32[1024]{0:T(1024)S(1)} %pad_clamp_fusion), kind=kCustom, calls=%fused_computation.1 | custom fusion | bytes 25167360 | tf_op jit(solution)/shard_map/jit(_take)/gather | solution.py:30
  258.0 7.9 %fusion = f32[6,4,128,128,1]{3,2,1,4,0:T(8,128)S(1)} fusion(bf16[6,16,4,128,128]{4,3,2,1,0:T(8,128)(2,1)} %bitcast.62, pred[6,16,4]{2,1,0:T(8,128)(4,1)S(1)} %copy.42, bf16[6,16,128,128]{3,2,1,0:T(8,128)(2,1)S(1)} %copy-done), kind=kOutput, calls=%fused_computation.3 | convolution fusion | flops 1616904192 | bytes 17301888 | tf_op jit(solution)/shard_map/aixy,aijyz->ajxz/dot_general | solution.py:56
  265.8 1.1 copy-done.1
  267.0 1.0 fusion.13
  268.0 51.2 %all-gather.2.cloned.1.call-done = bf16[6,16,128,128]{2,3,1,0:T(8,128)(2,1)} async-done(((bf16[6,4,128,128]{2,3,1,0:T(8,128)(2,1)}), bf16[6,16,128,128]{2,3,1,0:T(8,128)(2,1)}) %all-gather.2.cloned.1.call-update) | async-done | bytes 3145744 | tf_op jit(solution)/shard_map/all_gather | solution.py:58
  319.2 8.7 %fusion.10 = bf16[6,4,128,128]{2,3,1,0:T(8,128)(2,1)S(1)} fusion(bf16[6,16,128,128]{2,3,1,0:T(8,128)(2,1)} %all-gather.2.cloned.1.call-done, bf16[6,16,4,128,128]{4,3,2,1,0:T(8,128)(2,1)} %bitcast.63, pred[6,16,4]{2,1,0:T(8,128)(4,1)S(1)} %copy.42, f32[6,4,128,128,1]{3,2,1,4,0:T(8,128)} %copy-done.1), kind=kOutput, calls=%fused_computation.14 | convolution fusion | flops 1618477056 | bytes 18088320 | tf_op jit(solution)/shard_map/aixy,aijyz->ajxz/dot_general | solution.py:59
  327.9 1.2 copy.47
  (19 shorter events, 3.4 us)
Async XLA Ops:
  6.5 177.3 %copy-start = (bf16[6,16,128,128]{3,2,1,0:T(8,128)(2,1)S(1)}, bf16[6,16,128,128]{3,2,1,0:T(8,128)(2,1)}, u32[]{:S(2)}) copy-start(bf16[6,16,128,128]{3,2,1,0:T(8,128)(2,1)} %param.2) | copy-start | bytes 9437188
  6.5 312.6 %all-gather.2.cloned.1.call-start = ((), (), s32[]{:S(2)}) async-start(), calls=%async_computation | async-start | bytes 3932160 | tf_op jit(solution)/shard_map/all_gather | solution.py:58
  6.5 173.3 %collective-permute-start.1 = (bf16[6,16,128,128]{3,2,1,0:T(8,128)(2,1)}, bf16[6,16,128,128]{3,2,1,0:T(8,128)(2,1)}, u32[]{:S(2)}, u32[]{:S(2)}) collective-permute-start(bf16[6,16,128,128]{3,2,1,0:T(8,128)(2,1)} %param.2), channel_id=1, source_target_pairs={{0,4},{4,8},{8,12},{12,16},{16,20},{20,24},{24,28},{28,32},{32,36}... | collective-permute-start | bytes 9437192 | tf_op jit(solution)/shard_map/ppermute | solution.py:11
  11.2 174.7 %collective-permute-start.2 = (bf16[6,16,128,128]{3,2,1,0:T(8,128)(2,1)}, bf16[6,16,128,128]{3,2,1,0:T(8,128)(2,1)}, u32[]{:S(2)}, u32[]{:S(2)}) collective-permute-start(bf16[6,16,128,128]{3,2,1,0:T(8,128)(2,1)} %param.2), channel_id=1, source_target_pairs={{0,508},{4,0},{8,4},{12,8},{16,12},{20,16},{24,20},{28,24},{32,28}... | collective-permute-start | bytes 9437192 | tf_op jit(solution)/shard_map/ppermute | solution.py:11
  22.0 155.5 %collective-permute-start = (bf16[2,16,128,128]{3,2,1,0:T(8,128)(2,1)}, bf16[2,16,128,128]{3,2,1,0:T(8,128)(2,1)}, u32[]{:S(2)}, u32[]{:S(2)}) collective-permute-start(bf16[2,16,128,128]{3,2,1,0:T(8,128)(2,1)} %get-tuple-element.8), channel_id=1, source_target_pairs={{0,8},{4,12},{8,16},{12,20},{16,24},{20,28},{24,32},{28,36},{32,40... | collective-permute-start | bytes 3145736 | tf_op jit(solution)/shard_map/ppermute | solution.py:11
  23.9 216.2 %collective-permute-start.3 = (bf16[2,16,128,128]{3,2,1,0:T(8,128)(2,1)}, bf16[2,16,128,128]{3,2,1,0:T(8,128)(2,1)}, u32[]{:S(2)}, u32[]{:S(2)}) collective-permute-start(bf16[2,16,128,128]{3,2,1,0:T(8,128)(2,1)} %get-tuple-element.7), channel_id=1, source_target_pairs={{0,504},{4,508},{8,0},{12,4},{16,8},{20,12},{24,16},{28,20},{32,24... | collective-permute-start | bytes 3145736 | tf_op jit(solution)/shard_map/ppermute | solution.py:11
  265.8 1.1 copy-start.1
Sparse Core Ops, SparseCore 0:
  268.1 51.0 all-gather.1
where the time goes:
time: 336 us
  waiting for transfers between devices  240 us (71%)
  local copies, waits for them, and re-layouts  40.9 us (12%)
  starting transfers between devices  20.8 us (6%)
  matrix products  16.6 us (5%)
  between operations  13.5 us (4%)
  other arithmetic  4.28 us (1%)
    ppermute x4, waiting for transfers between devices, passed_along(): lax.ppermute(value, axis, [(i, (i + by) % peers) for i in range(peers)])  189 us
    all_gather x1, waiting for transfers between devices, local(): whole_square = lax.all_gather(square, 'depth', axis=1, tiled=True)  51.2 us
    ppermute x4, starting transfers between devices, passed_along(): lax.ppermute(value, axis, [(i, (i + by) % peers) for i in range(peers)])  20.8 us
    gather x1, local copies, waits for them, and re-layouts, matched_blocks(): return jnp.take(flat_blocks, flat_index, axis=0, mode='fill', fill_value=0)  15.5 us
    unnamed x9, local copies, waits for them, and re-layouts  14.4 us
    dot_general x1, matrix products, local(): jnp.einsum('aixy,aijyz->ajxz', whole_square, selected, preferred_element_...  8.72 us
    dot_general x1, matrix products, local(): jnp.einsum('aixy,aijyz->ajxz', values, selected, preferred_element_type=j...  7.87 us
  transfers between devices with their start and end apart: 5, of which 3 were waited for; matrix products, arithmetic and copies ran while one was open for 7% of the time, Pallas kernels for 0%

commit v1 on v0

v1 whole, which is shorter than its diff:
```python
import functools

import jax
import jax.numpy as jnp
from jax import lax
from jax.experimental import pallas as pl
from jax.experimental.pallas import tpu as pltpu
from jax.sharding import PartitionSpec as P

HB = 8
BAND = 2 * HB + 1
MESH = pl.DeviceIdType.MESH


def spread_kernel(off_ref, v_ref, o_ref):
    m = pl.program_id(0)
    slots, bs = v_ref.shape[1], v_ref.shape[2]
    o_ref[...] = jnp.zeros_like(o_ref)
    for s in range(slots):
        at = pl.multiple_of(off_ref[m, s] * bs, bs)
        o_ref[0, :, pl.ds(at, bs)] = v_ref[0, s]


def spread(off, values):
    rows, slots, bs, _ = values.shape
    return pl.pallas_call(
        spread_kernel,
        out_shape=jax.ShapeDtypeStruct((rows, bs, BAND * bs), values.dtype),
        grid_spec=pltpu.PrefetchScalarGridSpec(
            num_scalar_prefetch=1,
            grid=(rows,),
            in_specs=[pl.BlockSpec((1, slots, bs, bs), lambda m, off: (m, 0, 0, 0))],
            out_specs=pl.BlockSpec((1, bs, BAND * bs), lambda m, off: (m, 0, 0)),
        ),
    )(off, values)


def halo_rows(rows):
    frame = rows + 2 * HB
    listed = []
    for near in range(HB):
        for f in (HB - 1 - near, HB + rows + near):
            owner, m = (f - HB) // rows, (f - HB) % rows
            lo = max(0, HB - f)
            hi = min(2 * HB, frame - 1 + HB - f)
            listed.append((f, owner, m, lo, f + lo - HB, hi - lo + 1))
    return listed


def square_kernel(sizes, own_ref, field, square, own_sem, z_send, z_recv, x_send, x_recv, y_send, y_recv):
    nrow, ncol, layers = sizes
    rows, bs = own_ref.shape[0], own_ref.shape[1]
    frame = rows + 2 * HB
    groups = nrow * ncol
    strip = bs // layers
    half = strip // 2
    r, c, d = lax.axis_index("row"), lax.axis_index("col"), lax.axis_index("depth")
    g = r * ncol + c
    halo = halo_rows(rows)

    def group_at(by):
        t = lax.rem(g + by + groups, groups)
        return (lax.div(t, ncol), lax.rem(t, ncol), d)

    up, down = lax.rem(d + 1, layers), lax.rem(d + layers - 1, layers)
    beside = ((r, c, up), (r, c, down))
    owners = sorted({h[1] for h in halo})

    barrier = pltpu.get_barrier_semaphore()
    for by in owners:
        pl.semaphore_signal(barrier, inc=1, device_id=group_at(by), device_id_type=MESH)
    for peer in beside:
        pl.semaphore_signal(barrier, inc=1, device_id=peer, device_id_type=MESH)
    pl.semaphore_wait(barrier, len(owners) + 2)

    def part(k, layer, start, count):
        f, _, _, _, col, blocks = halo[k]
        first = pl.multiple_of(f * bs + layer * strip + start, half)
        return field.at[pl.ds(first, count), pl.ds(col * bs, blocks * bs)]

    def z_copy(k):
        f, owner, m, lo, col, blocks = halo[k]
        src = own_ref.at[m, pl.ds(pl.multiple_of(d * strip, strip), strip), pl.ds(lo * bs, blocks * bs)]
        return pltpu.make_async_remote_copy(
            src, part(k, d, 0, strip), z_send.at[k], z_recv.at[k], group_at(-owner), MESH
        )

    def x_copy(k, way):
        ref = part(k, d, 0, strip)
        return pltpu.make_async_remote_copy(ref, ref, x_send.at[way, k], x_recv.at[way, k], beside[way], MESH)

    def y_copy(k, way):
        ref = part(k, (down, up)[way], way * half, half)
        return pltpu.make_async_remote_copy(ref, ref, y_send.at[way, k], y_recv.at[way, k], beside[way], MESH)

    own_copies = [
        pltpu.make_async_copy(
            own_ref.at[m],
            field.at[pl.ds((HB + m) * bs, bs), pl.ds(m * bs, BAND * bs)],
            own_sem.at[m],
        )
        for m in range(rows)
    ]
    for k in range(len(halo)):
        z_copy(k).start()
    for copy in own_copies:
        copy.start()

    for f in range(frame):
        low, high = max(0, f - HB), min(frame, f + HB + 1)
        if low:
            field[pl.ds(f * bs, bs), pl.ds(0, low * bs)] = jnp.zeros((bs, low * bs), field.dtype)
        if high < frame:
            field[pl.ds(f * bs, bs), pl.ds(high * bs, (frame - high) * bs)] = jnp.zeros(
                (bs, (frame - high) * bs), field.dtype
            )
    square[...] = jnp.zeros_like(square)

    def add_pair(f):
        a0, a1 = max(0, f - 2 * HB), min(rows, f + 2)
        c0, c1 = max(0, f - HB), min(frame, f + HB + 2)
        left = field[pl.ds((HB + a0) * bs, (a1 - a0) * bs), pl.ds(f * bs, 2 * bs)]

        def body(t, _):
            at = pl.multiple_of((c0 + 2 * t) * bs, 2 * bs)
            right = field[pl.ds(f * bs, 2 * bs), pl.ds(at, 2 * bs)]
            square[pl.ds(a0 * bs, (a1 - a0) * bs), pl.ds(at, 2 * bs)] += jnp.dot(
                left, right, preferred_element_type=jnp.float32
            )
            return 0

        lax.fori_loop(0, (c1 - c0) // 2, body, 0)

    def second_hop(k):
        for way in range(2):
            x_copy(k, way).wait_recv()
            y_copy(k, way).start()

    def landed(f):
        for k in range(len(halo)):
            if halo[k][0] in (f, f + 1):
                for way in range(2):
                    y_copy(k, way).wait_recv()

    work = {}
    for p in range(rows // 2):
        work[p] = HB + 2 * p
    for p in range(HB // 2):
        work[5 + 4 * p] = HB - 2 - 2 * p
        work[6 + 4 * p] = HB + rows + 2 * p

    for t in range(7 + 4 * (HB // 2)):
        if t < len(halo):
            z_copy(t).wait_recv()
            for way in range(2):
                x_copy(t, way).start()
        if 1 <= t <= len(halo):
            second_hop(t - 1)
        if t in work:
            f = work[t]
            if t == 0:
                for copy in own_copies:
                    copy.wait()
            if not HB <= f < HB + rows:
                landed(f)
            add_pair(f)

    for k in range(len(halo)):
        z_copy(k).wait_send()
        for way in range(2):
            x_copy(k, way).wait_send()
            y_copy(k, way).wait_send()


def cube_kernel(off_ref, field, square, out_ref):
    rows, quarter, bs = out_ref.shape[:3]
    d = lax.axis_index("depth")
    slots = off_ref.shape[1]

    def cube_row(m, _):
        at = [pl.multiple_of((m + off_ref[m, s]) * bs, bs) for s in range(slots)]
        row = pl.ds(pl.multiple_of(m * bs, bs), bs)
        left = jnp.concatenate(
            [square[row, pl.ds(at[s], bs)].astype(field.dtype) for s in range(slots)], axis=1
        )
        for j in range(0, quarter, 2):
            to = [pl.multiple_of((m + off_ref[m, d * quarter + j + e]) * bs, bs) for e in range(2)]
            right = jnp.concatenate(
                [
                    jnp.concatenate([field[pl.ds(at[s], bs), pl.ds(to[e], bs)] for e in range(2)], axis=1)
                    for s in range(slots)
                ],
                axis=0,
            )
            cube = jnp.dot(left, right, preferred_element_type=jnp.float32)
            for e in range(2):
                out_ref[m, j + e] = (
                    3.0 * square[row, pl.ds(to[e], bs)] - 2.0 * cube[:, e * bs : (e + 1) * bs]
                ).astype(out_ref.dtype)
        return 0

    lax.fori_loop(0, rows, cube_row, 0)


def local(sizes, values, columns):
    rows, slots, bs, _ = values.shape
    total = columns.shape[0]
    layers = sizes[2]
    first = lax.axis_index(("row", "col")) * rows
    own_cols = lax.dynamic_slice_in_dim(columns, first, rows, 0)
    row_ids = first + jnp.arange(rows, dtype=jnp.int32)[:, None]
    off = jnp.mod(own_cols - row_ids + HB, total)
    own = spread(off, values)
    frame = rows + 2 * HB
    count = 2 * HB
    dma = pltpu.SemaphoreType.DMA
    vmem = pl.BlockSpec(memory_space=pltpu.VMEM)
    field, square = pl.pallas_call(
        functools.partial(square_kernel, sizes),
        out_shape=(
            pltpu.VMEM((frame * bs, frame * bs), values.dtype),
            pltpu.VMEM((rows * bs, frame * bs), jnp.float32),
        ),
        in_specs=[pl.BlockSpec(memory_space=pl.ANY)],
        out_specs=(vmem, vmem),
        scratch_shapes=[
            dma((rows,)),
            dma((count,)),
            dma((count,)),
            dma((2, count)),
            dma((2, count)),
            dma((2, count)),
            dma((2, count)),
        ],
        compiler_params=pltpu.CompilerParams(
            collective_id=0, has_side_effects=True, vmem_limit_bytes=4 * 1024 * 1024
        ),
    )(own)
    return pl.pallas_call(
        cube_kernel,
        out_shape=jax.ShapeDtypeStruct((rows, slots // layers, bs, bs), values.dtype),
        in_specs=[pl.BlockSpec(memory_space=pltpu.SMEM), vmem, vmem],
        out_specs=vmem,
        compiler_params=pltpu.CompilerParams(vmem_limit_bytes=4 * 1024 * 1024),
    )(off, field, square)


def solution(mesh):
    sizes = (mesh.shape["row"], mesh.shape["col"], mesh.shape["depth"])
    return jax.shard_map(
        functools.partial(local, sizes),
        mesh=mesh,
        in_specs=(P(("row", "col"), None, None, None), P()),
        out_specs=P(("row", "col"), "depth", None, None),
        check_vma=False,
    )
```

time: 336 us -> 93.7 us (0.28)
  the two profiles are of different devices: /device:TPU:1 before, /device:TPU:2 now
where the time goes in v1:
time: 93.7 us; the launch traced here: 93.4 us
  Pallas kernels  89.8 us (96%)
  local copies, waits for them, and re-layouts  2.9 us (3%)
    pallas_call x1, Pallas kernels, local(): pl.pallas_call(functools.partial(square_kernel, sizes), out_shape=(pltpu....  78.8 us
    pallas_call x1, Pallas kernels, spread(): pl.pallas_call(spread_kernel, out_shape=jax.ShapeDtypeStruct((rows, bs, B...  6.44 us
    pallas_call x1, Pallas kernels, local(): pl.pallas_call(cube_kernel, out_shape=jax.ShapeDtypeStruct((rows, slots /...  4.51 us
    unnamed x7, local copies, waits for them, and re-layouts  2.82 us

profile of v1, /device:TPU:2, one launch (start us, length us, event | category | flops | bytes accessed | tf_op | source)
XLA Modules:
  0.0 93.4 jit_solution(1498073980942693321)
XLA Ops:
  0.0 0.0 copy-start
  0.0 0.8 copy-done
  0.8 0.1 constant_dynamic-slice_fusion
  0.9 0.1 copy.4
  1.0 0.7 add_select_fusion.off_ref
  1.6 0.0 copy-start.2
  1.6 6.4 %shard_map.28.own_ref = bf16[6,128,2176]{2,1,0:T(8,128)(2,1)} custom-call(s32[6,16]{1,0:T(8,128)} %add_select_fusion.off_ref, bf16[6,16,128,128]{3,2,1,0:T(8,128)(2,1)} %v_ref.1), custom_call_target="tpu_custom_call" | custom-call | tf_op jit(solution)/shard_map/pallas_call | solution.py:26
  8.1 0.0 copy-start.1
  8.1 1.9 %copy-done.1 = bf16[6,128,2176]{2,1,0:T(8,128)(2,1)S(1)} copy-done((bf16[6,128,2176]{2,1,0:T(8,128)(2,1)S(1)}, bf16[6,128,2176]{2,1,0:T(8,128)(2,1)}, u32[]{:S(2)}) %copy-start.1) | copy-done | bytes 3342360
  10.0 78.8 %shard_map.29 = (bf16[2816,2816]{1,0:T(8,128)(2,1)S(1)}, f32[768,2816]{1,0:T(8,128)S(1)}) custom-call(bf16[6,128,2176]{2,1,0:T(8,128)(2,1)S(1)} %copy-done.1), custom_call_target="tpu_custom_call" | custom-call | tf_op jit(solution)/shard_map/pallas_call | solution.py:218
  88.9 0.0 copy-done.2
  88.9 4.5 %shard_map.30 = bf16[6,4,128,128]{3,2,1,0:T(8,128)(2,1)} custom-call(s32[6,16]{1,0:T(8,128)S(1)} %copy-done.2, bf16[2816,2816]{1,0:T(8,128)(2,1)S(1)} %get-tuple-element.7.field, f32[768,2816]{1,0:T(8,128)S(1)} %get-tuple-element.8.square), custom_call_target="tpu_custom_call" | custom-call | tf_op jit(solution)/shard_map/pallas_call | solution.py:239
  (1 shorter events, 0.0 us)
Async XLA Ops:
  0.0 0.8 copy-start
  1.6 87.2 %copy-start.2 = (s32[6,16]{1,0:T(8,128)S(1)}, s32[6,16]{1,0:T(8,128)}, u32[]{:S(2)}) copy-start(s32[6,16]{1,0:T(8,128)} %add_select_fusion.off_ref) | copy-start | bytes 1156
  8.1 1.9 %copy-start.1 = (bf16[6,128,2176]{2,1,0:T(8,128)(2,1)S(1)}, bf16[6,128,2176]{2,1,0:T(8,128)(2,1)}, u32[]{:S(2)}) copy-start(bf16[6,128,2176]{2,1,0:T(8,128)(2,1)} %shard_map.28.own_ref) | copy-start | bytes 10027012

commit v2 on v1

--- a/solution.py
+++ b/solution.py
@@ -12,26 +12,42 @@
 MESH = pl.DeviceIdType.MESH
 
 
-def spread_kernel(off_ref, v_ref, o_ref):
-    m = pl.program_id(0)
-    slots, bs = v_ref.shape[1], v_ref.shape[2]
-    o_ref[...] = jnp.zeros_like(o_ref)
-    for s in range(slots):
-        at = pl.multiple_of(off_ref[m, s] * bs, bs)
-        o_ref[0, :, pl.ds(at, bs)] = v_ref[0, s]
+def spread_kernel(off_ref, v_ref, o_ref, sem):
+    rows, slots, bs = v_ref.shape[:3]
+
+    def block(m, at):
+        return o_ref.at[m, :, pl.ds(pl.multiple_of(at * bs, bs), bs)]
+
+    def copy(m, s):
+        return pltpu.make_async_copy(v_ref.at[m, s], block(m, off_ref[m, s]), sem.at[m, s])
+
+    for m in range(rows):
+        for s in range(slots):
+            copy(m, s).start()
+    for m in range(rows):
+        absent = BAND * (BAND - 1) // 2
+        for s in range(slots):
+            absent = absent - off_ref[m, s]
+        at = pl.multiple_of(absent * bs, bs)
+        o_ref[m, :, pl.ds(at, bs)] = jnp.zeros((bs, bs), o_ref.dtype)
+    for m in range(rows):
+        for s in range(slots):
+            copy(m, s).wait()
 
 
 def spread(off, values):
     rows, slots, bs, _ = values.shape
+    assert slots == BAND - 1
     return pl.pallas_call(
         spread_kernel,
-        out_shape=jax.ShapeDtypeStruct((rows, bs, BAND * bs), values.dtype),
-        grid_spec=pltpu.PrefetchScalarGridSpec(
-            num_scalar_prefetch=1,
-            grid=(rows,),
-            in_specs=[pl.BlockSpec((1, slots, bs, bs), lambda m, off: (m, 0, 0, 0))],
-            out_specs=pl.BlockSpec((1, bs, BAND * bs), lambda m, off: (m, 0, 0)),
-        ),
+        out_shape=pltpu.VMEM((rows, bs, BAND * bs), values.dtype),
+        in_specs=[
+            pl.BlockSpec(memory_space=pltpu.SMEM),
+            pl.BlockSpec(memory_space=pltpu.HBM),
+        ],
+        out_specs=pl.BlockSpec(memory_space=pltpu.VMEM),
+        scratch_shapes=[pltpu.SemaphoreType.DMA((rows, slots))],
+        compiler_params=pltpu.CompilerParams(vmem_limit_bytes=58 * 1024 * 1024),
     )(off, values)
 
 
@@ -47,7 +63,7 @@
     return listed
 
 
-def square_kernel(sizes, own_ref, field, square, own_sem, z_send, z_recv, x_send, x_recv, y_send, y_recv):
+def square_kernel(sizes, own_ref, field, square, z_send, z_recv, w_send, w_recv, x_send, x_recv, y_send, y_recv):
     nrow, ncol, layers = sizes
     rows, bs = own_ref.shape[0], own_ref.shape[1]
     frame = rows + 2 * HB
@@ -64,14 +80,15 @@
 
     up, down = lax.rem(d + 1, layers), lax.rem(d + layers - 1, layers)
     beside = ((r, c, up), (r, c, down))
-    owners = sorted({h[1] for h in halo})
+    straight = (8, 9, 10, 11)
+    reach = sorted({h[1] for h in halo if abs(h[1]) == 1})
 
     barrier = pltpu.get_barrier_semaphore()
-    for by in owners:
+    for by in reach:
         pl.semaphore_signal(barrier, inc=1, device_id=group_at(by), device_id_type=MESH)
     for peer in beside:
         pl.semaphore_signal(barrier, inc=1, device_id=peer, device_id_type=MESH)
-    pl.semaphore_wait(barrier, len(owners) + 2)
+    pl.semaphore_wait(barrier, len(reach) + 2)
 
     def part(k, layer, start, count):
         f, _, _, _, col, blocks = halo[k]
@@ -80,10 +97,31 @@
 
     def z_copy(k):
         f, owner, m, lo, col, blocks = halo[k]
-        src = own_ref.at[m, pl.ds(pl.multiple_of(d * strip, strip), strip), pl.ds(lo * bs, blocks * bs)]
+        step = 1 if owner > 0 else -1
+        if owner == step:
+            rows_at = pl.ds(pl.multiple_of(d * strip, strip), strip)
+            src = own_ref.at[m, rows_at, pl.ds(lo * bs, blocks * bs)]
+        else:
+            first = pl.multiple_of((f - step * rows) * bs + d * strip, half)
+            src = field.at[pl.ds(first, strip), pl.ds((col - step * rows) * bs, blocks * bs)]
         return pltpu.make_async_remote_copy(
-            src, part(k, d, 0, strip), z_send.at[k], z_recv.at[k], group_at(-owner), MESH
+            src, part(k, d, 0, strip), z_send.at[k], z_recv.at[k], group_at(-step), MESH
         )
+
+    def w_copy(k):
+        f, owner, m, lo, col, blocks = halo[k]
+        q = lax.rem(d + layers // 2, layers)
+        rows_at = pl.ds(pl.multiple_of(q * strip, strip), strip)
+        src = own_ref.at[m, rows_at, pl.ds(lo * bs, blocks * bs)]
+        return pltpu.make_async_remote_copy(
+            src, part(k, q, 0, strip), w_send.at[k], w_recv.at[k], group_at(-owner), MESH
+        )
+
+    def relays(k):
+        f, owner = halo[k][:2]
+        for j in range(len(halo)):
+            if halo[j][1] == 2 * owner and halo[j][0] == f + owner * rows:
+                z_copy(j).start()
 
     def x_copy(k, way):
         ref = part(k, d, 0, strip)
@@ -93,20 +131,11 @@
         ref = part(k, (down, up)[way], way * half, half)
         return pltpu.make_async_remote_copy(ref, ref, y_send.at[way, k], y_recv.at[way, k], beside[way], MESH)
 
-    own_copies = [
-        pltpu.make_async_copy(
-            own_ref.at[m],
-            field.at[pl.ds((HB + m) * bs, bs), pl.ds(m * bs, BAND * bs)],
-            own_sem.at[m],
-        )
-        for m in range(rows)
-    ]
     for k in range(len(halo)):
-        z_copy(k).start()
-    for copy in own_copies:
-        copy.start()
-
-    for f in range(frame):
+        if abs(halo[k][1]) == 1:
+            z_copy(k).start()
+
+    def clear(f):
         low, high = max(0, f - HB), min(frame, f + HB + 1)
         if low:
             field[pl.ds(f * bs, bs), pl.ds(0, low * bs)] = jnp.zeros((bs, low * bs), field.dtype)
@@ -114,7 +143,15 @@
             field[pl.ds(f * bs, bs), pl.ds(high * bs, (frame - high) * bs)] = jnp.zeros(
                 (bs, (frame - high) * bs), field.dtype
             )
-    square[...] = jnp.zeros_like(square)
+
+    def place_own():
+        for m in range(rows):
+            field[pl.ds((HB + m) * bs, bs), pl.ds(m * bs, BAND * bs)] = own_ref[m]
+            clear(HB + m)
+        done = 2 * HB + 2
+        square[:, pl.ds(done * bs, (frame - done) * bs)] = jnp.zeros(
+            (rows * bs, (frame - done) * bs), square.dtype
+        )
 
     def add_pair(f):
         a0, a1 = max(0, f - 2 * HB), min(rows, f + 2)
@@ -124,9 +161,12 @@
         def body(t, _):
             at = pl.multiple_of((c0 + 2 * t) * bs, 2 * bs)
             right = field[pl.ds(f * bs, 2 * bs), pl.ds(at, 2 * bs)]
-            square[pl.ds(a0 * bs, (a1 - a0) * bs), pl.ds(at, 2 * bs)] += jnp.dot(
-                left, right, preferred_element_type=jnp.float32
-            )
+            term = jnp.dot(left, right, preferred_element_type=jnp.float32)
+            to = pl.ds(a0 * bs, (a1 - a0) * bs), pl.ds(at, 2 * bs)
+            if f == HB:
+                square[to] = term
+            else:
+                square[to] += term
             return 0
 
         lax.fori_loop(0, (c1 - c0) // 2, body, 0)
@@ -134,33 +174,43 @@
     def second_hop(k):
         for way in range(2):
             x_copy(k, way).wait_recv()
-            y_copy(k, way).start()
+            if k not in straight:
+                y_copy(k, way).start()
 
     def landed(f):
         for k in range(len(halo)):
             if halo[k][0] in (f, f + 1):
+                if k in straight:
+                    w_copy(k).wait_recv()
+                    continue
                 for way in range(2):
                     y_copy(k, way).wait_recv()
 
-    work = {}
-    for p in range(rows // 2):
-        work[p] = HB + 2 * p
+    lag = 2
+    work = {p: HB + 2 * p for p in range(rows // 2)}
     for p in range(HB // 2):
-        work[5 + 4 * p] = HB - 2 - 2 * p
-        work[6 + 4 * p] = HB + rows + 2 * p
-
-    for t in range(7 + 4 * (HB // 2)):
+        work[6 + 4 * p] = HB - 2 - 2 * p
+        work[7 + 4 * p] = HB + rows + 2 * p
+
+    for t in range(8 + 4 * (HB // 2)):
         if t < len(halo):
             z_copy(t).wait_recv()
             for way in range(2):
                 x_copy(t, way).start()
-        if 1 <= t <= len(halo):
-            second_hop(t - 1)
+            relays(t)
+            if t == 3:
+                for k in straight:
+                    w_copy(k).start()
+        if lag <= t < len(halo) + lag:
+            second_hop(t - lag)
+        if t == 0:
+            place_own()
+        if 1 <= t <= HB // 2:
+            for f in (2 * t - 2, 2 * t - 1):
+                clear(f)
+                clear(HB + rows + f)
         if t in work:
             f = work[t]
-            if t == 0:
-                for copy in own_copies:
-                    copy.wait()
             if not HB <= f < HB + rows:
                 landed(f)
             add_pair(f)
@@ -169,7 +219,10 @@
         z_copy(k).wait_send()
         for way in range(2):
             x_copy(k, way).wait_send()
-            y_copy(k, way).wait_send()
+            if k not in straight:
+                y_copy(k, way).wait_send()
+        if k in straight:
+            w_copy(k).wait_send()
 
 
 def cube_kernel(off_ref, field, square, out_ref):
@@ -221,10 +274,11 @@
             pltpu.VMEM((frame * bs, frame * bs), values.dtype),
             pltpu.VMEM((rows * bs, frame * bs), jnp.float32),
         ),
-        in_specs=[pl.BlockSpec(memory_space=pl.ANY)],
+        in_specs=[vmem],
         out_specs=(vmem, vmem),
         scratch_shapes=[
-            dma((rows,)),
+            dma((count,)),
+            dma((count,)),
             dma((count,)),
             dma((count,)),
             dma((2, count)),

time: 93.7 us -> 82.7 us (0.88)
  the two profiles are of different devices: /device:TPU:2 before, /device:TPU:34 now
where the time goes in v2:
time: 82.7 us; the launch traced here: 82.4 us
  Pallas kernels  80.8 us (98%)
  local copies, waits for them, and re-layouts  0.95 us (1%)
    pallas_call x1, Pallas kernels, local(): pl.pallas_call(functools.partial(square_kernel, sizes), out_shape=(pltpu....  72.7 us
    pallas_call x1, Pallas kernels, local(): pl.pallas_call(cube_kernel, out_shape=jax.ShapeDtypeStruct((rows, slots /...  4.49 us
    pallas_call x1, Pallas kernels, spread(): pl.pallas_call(spread_kernel, out_shape=pltpu.VMEM((rows, bs, BAND * bs),...  3.53 us

profile of v2, /device:TPU:34, one launch (start us, length us, event | category | flops | bytes accessed | tf_op | source)
XLA Modules:
  0.0 82.4 jit_solution(110193815645733488)
XLA Ops:
  0.0 0.0 copy-start
  0.0 0.8 copy-done
  0.8 0.1 constant_dynamic-slice_fusion
  0.9 0.1 copy.4
  1.0 0.7 add_select_fusion.off_ref
  1.6 0.0 copy-start.1
  1.6 3.5 %shard_map.28.own_ref = bf16[6,128,2176]{2,1,0:T(8,128)(2,1)S(1)} custom-call(s32[6,16]{1,0:T(8,128)} %add_select_fusion.off_ref, bf16[6,16,128,128]{3,2,1,0:T(8,128)(2,1)} %v_ref.1), custom_call_target="tpu_custom_call" | custom-call | tf_op jit(solution)/shard_map/pallas_call | solution.py:41
  5.2 72.7 %shard_map.29 = (bf16[2816,2816]{1,0:T(8,128)(2,1)S(1)}, f32[768,2816]{1,0:T(8,128)S(1)}) custom-call(bf16[6,128,2176]{2,1,0:T(8,128)(2,1)S(1)} %shard_map.28.own_ref), custom_call_target="tpu_custom_call" | custom-call | tf_op jit(solution)/shard_map/pallas_call | solution.py:271
  77.9 0.0 copy-done.1
  77.9 4.5 %shard_map.30 = bf16[6,4,128,128]{3,2,1,0:T(8,128)(2,1)} custom-call(s32[6,16]{1,0:T(8,128)S(1)} %copy-done.1, bf16[2816,2816]{1,0:T(8,128)(2,1)S(1)} %get-tuple-element.7.field, f32[768,2816]{1,0:T(8,128)S(1)} %get-tuple-element.8.square), custom_call_target="tpu_custom_call" | custom-call | tf_op jit(solution)/shard_map/pallas_call | solution.py:293
  (1 shorter events, 0.0 us)
Async XLA Ops:
  0.0 0.8 copy-start
  1.6 76.3 %copy-start.1 = (s32[6,16]{1,0:T(8,128)S(1)}, s32[6,16]{1,0:T(8,128)}, u32[]{:S(2)}) copy-start(s32[6,16]{1,0:T(8,128)} %add_select_fusion.off_ref) | copy-start | bytes 1156

commit v3 on v2

--- a/solution.py
+++ b/solution.py
@@ -54,7 +54,7 @@
 def halo_rows(rows):
     frame = rows + 2 * HB
     listed = []
-    for near in range(HB):
+    for near in (*range(HB - 4), HB - 2, HB - 1, HB - 4, HB - 3):
         for f in (HB - 1 - near, HB + rows + near):
             owner, m = (f - HB) // rows, (f - HB) % rows
             lo = max(0, HB - f)
@@ -80,7 +80,7 @@
 
     up, down = lax.rem(d + 1, layers), lax.rem(d + layers - 1, layers)
     beside = ((r, c, up), (r, c, down))
-    straight = (8, 9, 10, 11)
+    straight = tuple(range(len(halo) - 4, len(halo)))
     reach = sorted({h[1] for h in halo if abs(h[1]) == 1})
 
     barrier = pltpu.get_barrier_semaphore()
@@ -132,7 +132,7 @@
         return pltpu.make_async_remote_copy(ref, ref, y_send.at[way, k], y_recv.at[way, k], beside[way], MESH)
 
     for k in range(len(halo)):
-        if abs(halo[k][1]) == 1:
+        if abs(halo[k][1]) == 1 and k not in straight:
             z_copy(k).start()
 
     def clear(f):
@@ -188,17 +188,19 @@
 
     lag = 2
     work = {p: HB + 2 * p for p in range(rows // 2)}
-    for p in range(HB // 2):
-        work[6 + 4 * p] = HB - 2 - 2 * p
-        work[7 + 4 * p] = HB + rows + 2 * p
-
-    for t in range(8 + 4 * (HB // 2)):
+    for p, t in zip((0, 1, 3, 2), (6, 10, 14, 17)):
+        work[t] = HB - 2 - 2 * p
+        work[t + 1] = HB + rows + 2 * p
+
+    for t in range(len(halo) + 3):
         if t < len(halo):
             z_copy(t).wait_recv()
             for way in range(2):
                 x_copy(t, way).start()
             relays(t)
             if t == 3:
+                for k in straight:
+                    z_copy(k).start()
                 for k in straight:
                     w_copy(k).start()
         if lag <= t < len(halo) + lag:

time: 82.7 us -> 81.4 us (0.984)
  the two profiles are of different devices: /device:TPU:34 before, /device:TPU:1 now
where the time goes in v3:
time: 81.4 us; the launch traced here: 81 us
  Pallas kernels  79.3 us (97%)
  local copies, waits for them, and re-layouts  0.95 us (1%)
    pallas_call x1, Pallas kernels, local(): pl.pallas_call(functools.partial(square_kernel, sizes), out_shape=(pltpu....  71.3 us
    pallas_call x1, Pallas kernels, local(): pl.pallas_call(cube_kernel, out_shape=jax.ShapeDtypeStruct((rows, slots /...  4.49 us
    pallas_call x1, Pallas kernels, spread(): pl.pallas_call(spread_kernel, out_shape=pltpu.VMEM((rows, bs, BAND * bs),...  3.53 us

profile of v3, /device:TPU:1, one launch (start us, length us, event | category | flops | bytes accessed | tf_op | source)
XLA Modules:
  0.0 81.0 jit_solution(9379709478089607515)
XLA Ops:
  0.0 0.0 copy-start
  0.0 0.8 copy-done
  0.8 0.1 constant_dynamic-slice_fusion
  0.9 0.1 copy.4
  1.0 0.7 add_select_fusion.off_ref
  1.6 0.0 copy-start.1
  1.6 3.5 %shard_map.28.own_ref = bf16[6,128,2176]{2,1,0:T(8,128)(2,1)S(1)} custom-call(s32[6,16]{1,0:T(8,128)} %add_select_fusion.off_ref, bf16[6,16,128,128]{3,2,1,0:T(8,128)(2,1)} %v_ref.1), custom_call_target="tpu_custom_call" | custom-call | tf_op jit(solution)/shard_map/pallas_call | solution.py:41
  5.2 71.3 %shard_map.29 = (bf16[2816,2816]{1,0:T(8,128)(2,1)S(1)}, f32[768,2816]{1,0:T(8,128)S(1)}) custom-call(bf16[6,128,2176]{2,1,0:T(8,128)(2,1)S(1)} %shard_map.28.own_ref), custom_call_target="tpu_custom_call" | custom-call | tf_op jit(solution)/shard_map/pallas_call | solution.py:273
  76.5 0.0 copy-done.1
  76.5 4.5 %shard_map.30 = bf16[6,4,128,128]{3,2,1,0:T(8,128)(2,1)} custom-call(s32[6,16]{1,0:T(8,128)S(1)} %copy-done.1, bf16[2816,2816]{1,0:T(8,128)(2,1)S(1)} %get-tuple-element.7.field, f32[768,2816]{1,0:T(8,128)S(1)} %get-tuple-element.8.square), custom_call_target="tpu_custom_call" | custom-call | tf_op jit(solution)/shard_map/pallas_call | solution.py:295
  (1 shorter events, 0.0 us)
Async XLA Ops:
  0.0 0.8 copy-start
  1.6 74.8 %copy-start.1 = (s32[6,16]{1,0:T(8,128)S(1)}, s32[6,16]{1,0:T(8,128)}, u32[]{:S(2)}) copy-start(s32[6,16]{1,0:T(8,128)} %add_select_fusion.off_ref) | copy-start | bytes 1156

commit v4 on v3

--- a/solution.py
+++ b/solution.py
@@ -186,13 +186,13 @@
                 for way in range(2):
                     y_copy(k, way).wait_recv()
 
-    lag = 2
-    work = {p: HB + 2 * p for p in range(rows // 2)}
-    for p, t in zip((0, 1, 3, 2), (6, 10, 14, 17)):
-        work[t] = HB - 2 - 2 * p
-        work[t + 1] = HB + rows + 2 * p
-
-    for t in range(len(halo) + 3):
+    lag = 3
+    work = {1 + 2 * p: HB + 2 * p for p in range(rows // 2)}
+    for p, t in zip((0, 1, 3, 2), ((9, 11), (15, 16), (17, 18), (19, 20))):
+        work[t[0]] = HB - 2 - 2 * p
+        work[t[1]] = HB + rows + 2 * p
+
+    for t in range(len(halo) + 5):
         if t < len(halo):
             z_copy(t).wait_recv()
             for way in range(2):

time: 81.4 us -> 81.6 us (level)
  no operation moved by 1% of the time
where the time goes in v4:
time: 81.6 us; the launch traced here: 81.2 us
  Pallas kernels  79.5 us (97%)
  local copies, waits for them, and re-layouts  0.95 us (1%)
    pallas_call x1, Pallas kernels, local(): pl.pallas_call(functools.partial(square_kernel, sizes), out_shape=(pltpu....  71.6 us
    pallas_call x1, Pallas kernels, local(): pl.pallas_call(cube_kernel, out_shape=jax.ShapeDtypeStruct((rows, slots /...  4.44 us
    pallas_call x1, Pallas kernels, spread(): pl.pallas_call(spread_kernel, out_shape=pltpu.VMEM((rows, bs, BAND * bs),...  3.53 us

profile of v4, /device:TPU:1, one launch (start us, length us, event | category | flops | bytes accessed | tf_op | source)
XLA Modules:
  0.0 81.2 jit_solution(13029557189641590327)
XLA Ops:
  0.0 0.0 copy-start
  0.0 0.8 copy-done
  0.8 0.1 constant_dynamic-slice_fusion
  0.9 0.1 copy.4
  1.0 0.7 add_select_fusion.off_ref
  1.6 0.0 copy-start.1
  1.6 3.5 %shard_map.28.own_ref = bf16[6,128,2176]{2,1,0:T(8,128)(2,1)S(1)} custom-call(s32[6,16]{1,0:T(8,128)} %add_select_fusion.off_ref, bf16[6,16,128,128]{3,2,1,0:T(8,128)(2,1)} %v_ref.1), custom_call_target="tpu_custom_call" | custom-call | tf_op jit(solution)/shard_map/pallas_call | solution.py:41
  5.2 71.6 %shard_map.29 = (bf16[2816,2816]{1,0:T(8,128)(2,1)S(1)}, f32[768,2816]{1,0:T(8,128)S(1)}) custom-call(bf16[6,128,2176]{2,1,0:T(8,128)(2,1)S(1)} %shard_map.28.own_ref), custom_call_target="tpu_custom_call" | custom-call | tf_op jit(solution)/shard_map/pallas_call | solution.py:273
  76.8 0.0 copy-done.1
  76.8 4.4 %shard_map.30 = bf16[6,4,128,128]{3,2,1,0:T(8,128)(2,1)} custom-call(s32[6,16]{1,0:T(8,128)S(1)} %copy-done.1, bf16[2816,2816]{1,0:T(8,128)(2,1)S(1)} %get-tuple-element.7.field, f32[768,2816]{1,0:T(8,128)S(1)} %get-tuple-element.8.square), custom_call_target="tpu_custom_call" | custom-call | tf_op jit(solution)/shard_map/pallas_call | solution.py:295
  (1 shorter events, 0.0 us)
Async XLA Ops:
  0.0 0.8 copy-start
  1.6 75.1 %copy-start.1 = (s32[6,16]{1,0:T(8,128)S(1)}, s32[6,16]{1,0:T(8,128)}, u32[]{:S(2)}) copy-start(s32[6,16]{1,0:T(8,128)} %add_select_fusion.off_ref) | copy-start | bytes 1156
